TPU v7x, 32 devices: a whole 2x2x4 slice. The times are simulated.
32 devices in a mesh: bl: 8 (over y, x, core), ch: 4 (over z).
Axes of the slice: x: 2, y: 2, z: 4, core: 2. Of those that a mesh axis runs over, the one named last changes fastest.
Arguments:
- measured_correlations: float32 [2, 64, 16384], P(None, 'ch', 'bl'), may hold values from -6 to 6
- source_model_terms: float32 [2, 16, 64, 16384], P(None, None, 'ch', 'bl'), may hold values from -0.75 to 0.75
- stations: int32 [2, 16384], P(None, 'bl'), may hold values from 0 to 511, as said below
- initial_gains: float32 [2, 16, 64, 512], P(None, None, 'ch'), may hold values from -4 to 4
Outputs:
- gains: float32 [2, 16, 64, 512], P(None, None, 'ch')
- consensus: float32 [2, 16, 64, 512], P(None, None, 'ch')
Inputs may be any that keep to these rules, and one draw needn't show every extreme that they name: Each baseline joins two different stations.
All inputs are finite; a program needn't handle non-finite values.
Results may differ from a plain program's by a relative error of at most 0.00025.
Values sent between devices are 32-bit elements; how exact they have to be, the bound alone decides.
A program may use at most 64 MiB of HBM per device.

v0:
```python
import functools

import jax
import jax.numpy as jnp
import numpy as np
from jax import lax
from jax.experimental import pallas as pl
from jax.experimental.pallas import tpu as pltpu
from jax.sharding import PartitionSpec as P

SPECTRAL_BINS = 64
ITERS = 3
penalty = 1.0
MESH = pl.DeviceIdType.MESH
BLOCK = 512


def legendre_basis(channel_count):
    abscissa = -1.0 + 2.0 * jnp.arange(channel_count, dtype=jnp.float32) / (channel_count - 1)
    columns = []
    for degree in range(4):
        vector = abscissa**degree
        for earlier in columns:
            vector = vector - jnp.sum(earlier * vector) * earlier
        vector = vector / jnp.sqrt(jnp.sum(vector * vector))
        columns.append(vector)
    return jnp.stack(columns, axis=1)


def split(value):
    high = value.astype(jnp.bfloat16)
    return high, (value - high.astype(jnp.float32)).astype(jnp.bfloat16)


def totals_kernel(
    n_chunks, n_dir, n_chan, vis_ref, model_ref, row_ref, col_ref, gains_ref, out_ref,
    pieces, gain_l, gain_r, terms, back, accum,
):
    step = pl.program_id(0)
    rows = n_dir * n_chan
    chunk = rows // n_chunks
    block = vis_ref.shape[2]
    n_st = pieces.shape[1]
    half = n_st // 2

    @pl.when(step == 0)
    def _():
        for h in range(2):
            for c in range(n_chunks):
                for part in range(2):
                    high, low = split(gains_ref[h, c, pl.ds(part * chunk, chunk), :])
                    base = part * rows + c * chunk
                    pieces[pl.ds(base, chunk), pl.ds(h * half, half)] = high
                    pieces[pl.ds(2 * rows + base, chunk), pl.ds(h * half, half)] = low

    station = lax.broadcasted_iota(jnp.int32, (n_st, block), 0)
    hot_l = (station == row_ref[0:1, :]).astype(jnp.float32).astype(jnp.bfloat16)
    hot_r = (station == row_ref[1:2, :]).astype(jnp.float32).astype(jnp.bfloat16)
    for hot, gain in ((hot_l, gain_l), (hot_r, gain_r)):
        both = jnp.dot(pieces[...], hot, preferred_element_type=jnp.float32)
        gain[...] = both[: 2 * rows] + both[2 * rows :]

    def at(ref, part, d):
        return ref[pl.ds(part * rows + d * n_chan, n_chan), :]

    res_re = vis_ref[0]
    res_im = vis_ref[1]
    for d in range(n_dir):
        m_re, m_im = model_ref[0, d], model_ref[1, d]
        l_re, l_im = at(gain_l, 0, d), at(gain_l, 1, d)
        r_re, r_im = at(gain_r, 0, d), at(gain_r, 1, d)
        a_re = m_re * r_re + m_im * r_im
        a_im = m_im * r_re - m_re * r_im
        res_re = res_re - (l_re * a_re - l_im * a_im)
        res_im = res_im - (l_re * a_im + l_im * a_re)
    for d in range(n_dir):
        m_re, m_im = model_ref[0, d], model_ref[1, d]
        t_re = res_re * m_re + res_im * m_im
        t_im = res_re * m_im - res_im * m_re
        power = m_re * m_re + m_im * m_im
        for side, gain in ((0, gain_r), (1, gain_l)):
            g_re, g_im = at(gain, 0, d), at(gain, 1, d)
            sign = -1.0 if side == 0 else 1.0
            s_im = sign * t_im
            values = (
                t_re * g_re - s_im * g_im,
                t_re * g_im + s_im * g_re,
                power * (g_re * g_re + g_im * g_im),
            )
            for q, value in enumerate(values):
                high, low = split(value)
                base = q * rows + d * n_chan
                terms[pl.ds(base, n_chan), pl.ds(pl.multiple_of((step * 2 + side) * block, 128), block)] = high
                terms[pl.ds(3 * rows + base, n_chan), pl.ds(pl.multiple_of((step * 2 + side) * block, 128), block)] = low

    ids = lax.broadcasted_iota(jnp.int32, (block, n_st), 1)
    back_l = (ids == col_ref[:, 0:1]).astype(jnp.float32).astype(jnp.bfloat16)
    back_r = (ids == col_ref[:, 1:2]).astype(jnp.float32).astype(jnp.bfloat16)
    back[pl.ds(step * 2 * block, block), :] = back_l
    back[pl.ds(step * 2 * block + block, block), :] = back_r

    @pl.when(step == pl.num_programs(0) - 1)
    def _():
        accum[...] = jnp.dot(terms[...], back[...], preferred_element_type=jnp.float32)
        for h in range(2):
            for c in range(n_chunks):
                for q in range(3):
                    base = q * rows + c * chunk
                    out_ref[h, c, pl.ds(q * chunk, chunk), :] = (
                        accum[pl.ds(base, chunk), pl.ds(h * half, half)]
                        + accum[pl.ds(3 * rows + base, chunk), pl.ds(h * half, half)]
                    )


def local_totals(vis, model, ids, ids_t, gains, n_chunks):
    n_dir, n_chan, n_base = model.shape[1:]
    n_st = gains.shape[3] * 2
    rows = n_dir * n_chan
    chunk = rows // n_chunks
    block = min(BLOCK, n_base)
    return pl.pallas_call(
        functools.partial(totals_kernel, n_chunks, n_dir, n_chan),
        grid=(n_base // block,),
        out_shape=jax.ShapeDtypeStruct((2, n_chunks, 3 * chunk, n_st // 2), jnp.float32),
        in_specs=[
            pl.BlockSpec((2, n_chan, block), lambda i: (0, 0, i)),
            pl.BlockSpec((2, n_dir, n_chan, block), lambda i: (0, 0, 0, i)),
            pl.BlockSpec((2, block), lambda i: (0, i)),
            pl.BlockSpec((block, 2), lambda i: (i, 0)),
            pl.BlockSpec(gains.shape, lambda i: (0, 0, 0, 0)),
        ],
        out_specs=pl.BlockSpec((2, n_chunks, 3 * chunk, n_st // 2), lambda i: (0, 0, 0, 0)),
        scratch_shapes=[
            pltpu.VMEM((4 * rows, n_st), jnp.bfloat16),
            pltpu.VMEM((2 * rows, block), jnp.float32),
            pltpu.VMEM((2 * rows, block), jnp.float32),
            pltpu.VMEM((6 * rows, 2 * n_base), jnp.bfloat16),
            pltpu.VMEM((2 * n_base, n_st), jnp.bfloat16),
            pltpu.VMEM((6 * rows, n_st), jnp.float32),
        ],
        compiler_params=pltpu.CompilerParams(vmem_limit_bytes=56 * 2**20),
        name="station_totals",
    )(vis, model, ids, ids_t, gains)


def orders(n_bits):
    upper = list(range(1, n_bits))
    return ([0] + upper, [0] + upper[::-1])


def exchange_kernel(
    last, n_bits, n_ch, part_ref, state_ref, basis_ref, gains_ref, out_state_ref, coef_all_ref,
    acc, recv, coefs, sem_in, rs_send, rs_recv, ag_send, ag_recv, c_send, c_recv, k_send, k_recv,
):
    n = 2**n_bits
    rows = state_ref.shape[2]
    me = lax.axis_index("bl")
    ch = lax.axis_index("ch")
    bits = [lax.rem(me // (2**k), 2) for k in range(n_bits)]
    partners = [me + (1 - 2 * bits[k]) * (2**k) for k in range(n_bits)]
    load = pltpu.make_async_copy(part_ref, acc, sem_in)
    load.start()

    barrier = pltpu.get_barrier_semaphore()
    for k in range(n_bits):
        pl.semaphore_signal(barrier, inc=1, device_id=(partners[k], ch), device_id_type=MESH)
    for j in range(1, n_ch):
        pl.semaphore_signal(
            barrier, inc=1, device_id=(me, lax.rem(ch + j, n_ch)), device_id_type=MESH
        )
    pl.semaphore_wait(barrier, n_bits + n_ch - 1)
    load.wait()

    order = orders(n_bits)

    def region(stream, stage, flip):
        idx = [slice(None)] * n_bits
        for j in range(stage):
            k = order[stream][j]
            idx[n_bits - 1 - k] = bits[k]
        k = order[stream][stage]
        idx[n_bits - 1 - k] = (1 - bits[k]) if flip else bits[k]
        return (stream,) + tuple(idx)

    def rs_copy(stream, stage):
        k = order[stream][stage]
        slot = recv[stage].at[stream]
        return pltpu.make_async_remote_copy(
            src_ref=acc.at[region(stream, stage, True)],
            dst_ref=slot,
            send_sem=rs_send.at[stream, stage],
            recv_sem=rs_recv.at[stream, stage],
            device_id=(partners[k], ch),
            device_id_type=MESH,
        )

    copies = {}
    for s in range(2):
        copies[s, 0] = rs_copy(s, 0)
        copies[s, 0].start()
    for stage in range(n_bits):
        for s in range(2):
            copies[s, stage].wait_recv()
            where = region(s, stage, False)
            acc[where] = acc[where] + recv[stage][s]
            if stage + 1 < n_bits:
                copies[s, stage + 1] = rs_copy(s, stage + 1)
                copies[s, stage + 1].start()

    mine = tuple(bits[n_bits - 1 - i] for i in range(n_bits))

    def gather_copy(buf, sends, recvs, stream, stage):
        k = order[stream][stage]
        idx = [slice(None)] * n_bits
        for j in range(stage + 1):
            kk = order[stream][j]
            idx[n_bits - 1 - kk] = bits[kk]
        where = (stream,) + tuple(idx)
        return pltpu.make_async_remote_copy(
            src_ref=buf.at[where],
            dst_ref=buf.at[where],
            send_sem=sends.at[stream, stage],
            recv_sem=recvs.at[stream, stage],
            device_id=(partners[k], ch),
            device_id_type=MESH,
        )

    gathers = {}
    shifted = []
    for s in range(2):
        totals = acc[(s,) + mine]
        weight = totals[2 * rows :]
        factor = 1.0 / (weight + penalty)
        for part in range(2):
            gain = state_ref[0, s * 2 + part]
            cons = state_ref[1, s * 2 + part]
            dual = state_ref[2, s * 2 + part]
            numerator = totals[part * rows : (part + 1) * rows] + gain * weight
            new = (numerator + penalty * (cons - dual)) * factor
            gains_ref[(s,) + mine + (pl.ds(part * rows, rows),)] = new
            out_state_ref[0, s * 2 + part] = new
            shifted.append(new + dual)
        gathers[s, n_bits - 1] = gather_copy(gains_ref, ag_send, ag_recv, s, n_bits - 1)
        gathers[s, n_bits - 1].start()

    n_chan = basis_ref.shape[1]
    per = rows // n_chan
    for k in range(4):
        pieces = []
        for value in shifted:
            for i in range(per):
                pieces.append(
                    jnp.sum(
                        value[i * n_chan : (i + 1) * n_chan] * basis_ref[k], axis=0, keepdims=True
                    )
                )
        for r, piece in enumerate(pieces):
            coefs[0, k, pl.ds(r, 1), :] = piece
    sends = []
    for j in range(1, n_ch):
        copy = pltpu.make_async_remote_copy(
            src_ref=coefs.at[0],
            dst_ref=coefs.at[j],
            send_sem=c_send.at[j - 1],
            recv_sem=c_recv.at[j - 1],
            device_id=(me, lax.rem(ch + j, n_ch)),
            device_id_type=MESH,
        )
        copy.start()
        sends.append(copy)

    def advance(buf, sends, recvs, table, stage):
        for s in range(2):
            table[s, stage].wait_recv()
            if stage > 0:
                table[s, stage - 1] = gather_copy(buf, sends, recvs, s, stage - 1)
                table[s, stage - 1].start()

    advance(gains_ref, ag_send, ag_recv, gathers, n_bits - 1)
    for copy in sends:
        copy.wait_recv()
    total = [None] * 4
    for k in range(4):
        value = coefs[0, k]
        for j in range(1, n_ch):
            value = value + coefs[j, k]
        total[k] = value
    k_gathers = {}
    if last:
        for s in range(2):
            for k in range(4):
                coef_all_ref[(s,) + mine + (k,)] = total[k][s * 2 * per : (s + 1) * 2 * per]
            k_gathers[s, n_bits - 1] = gather_copy(coef_all_ref, k_send, k_recv, s, n_bits - 1)
            k_gathers[s, n_bits - 1].start()
        out_state_ref[1] = out_state_ref[0]
        out_state_ref[2] = out_state_ref[0]
    else:
        coef_all_ref[...] = jnp.zeros_like(coef_all_ref)
        for index, value in enumerate(shifted):
            for i in range(per):
                fit = total[0][index * per + i : index * per + i + 1] * basis_ref[0]
                for k in range(1, 4):
                    fit = fit + total[k][index * per + i : index * per + i + 1] * basis_ref[k]
                where = pl.ds(i * n_chan, n_chan)
                out_state_ref[1, index, where, :] = fit
                out_state_ref[2, index, where, :] = value[i * n_chan : (i + 1) * n_chan] - fit
    for stage in range(n_bits - 2, -1, -1):
        advance(gains_ref, ag_send, ag_recv, gathers, stage)
        if last:
            advance(coef_all_ref, k_send, k_recv, k_gathers, stage + 1)
    if last:
        advance(coef_all_ref, k_send, k_recv, k_gathers, 0)

    for table in (copies, gathers, k_gathers):
        for copy in table.values():
            copy.wait_send()
    for copy in sends:
        copy.wait_send()


def exchange(partial, state, basis, last, n, n_ch):
    n_bits = n.bit_length() - 1
    rows, half = state.shape[2:]
    n_chan = basis.shape[1]
    per = rows // n_chan
    twos = (2,) * n_bits
    partial = partial.reshape((2,) + twos + partial.shape[2:])
    coef_shape = (2,) + ((twos) if last else (1,) * n_bits) + (4, 2 * per, half)
    recv = [
        pltpu.VMEM((2,) + (2,) * (n_bits - 1 - stage) + (3 * rows, half), jnp.float32)
        for stage in range(n_bits)
    ]

    def body(part_ref, state_ref, basis_ref, gains_ref, out_state_ref, coef_all_ref, acc, *rest):
        return exchange_kernel(
            last, n_bits, n_ch, part_ref, state_ref, basis_ref, gains_ref, out_state_ref,
            coef_all_ref, acc, rest[:n_bits], *rest[n_bits:]
        )

    dma = pltpu.SemaphoreType.DMA
    vmem = pl.BlockSpec(memory_space=pltpu.VMEM)
    gains, state, coefs = pl.pallas_call(
        body,
        out_shape=(
            jax.ShapeDtypeStruct((2,) + twos + (2 * rows, half), jnp.float32),
            jax.ShapeDtypeStruct(state.shape, jnp.float32),
            jax.ShapeDtypeStruct(coef_shape, jnp.float32),
        ),
        in_specs=[pl.BlockSpec(memory_space=pl.ANY), vmem, vmem],
        out_specs=(vmem, vmem, vmem),
        scratch_shapes=[pltpu.VMEM(partial.shape, jnp.float32)]
        + recv
        + [
            pltpu.VMEM((n_ch, 4, 4 * per, half), jnp.float32),
            dma,
            dma((2, n_bits)),
            dma((2, n_bits)),
            dma((2, n_bits)),
            dma((2, n_bits)),
            dma((n_ch - 1,)),
            dma((n_ch - 1,)),
            dma((2, n_bits)),
            dma((2, n_bits)),
        ],
        compiler_params=pltpu.CompilerParams(
            collective_id=1 if last else 0,
            has_side_effects=True,
            vmem_limit_bytes=40 * 2**20,
        ),
        name="exchange_last" if last else "exchange",
    )(partial, state, basis)
    return gains.reshape((2, n, 2 * rows, half)), state, coefs


def per_device(n, n_ch, vis, model, stations, initial_gains):
    n_dir, n_chan, n_st = initial_gains.shape[1:]
    per = n_dir // n
    half = n_st // 2
    rows = per * n_chan
    chunks = initial_gains.reshape(2, n, rows, 2, half).transpose(3, 1, 0, 2, 4)
    me = lax.axis_index("bl")
    own = lax.dynamic_slice_in_dim(chunks, me, 1, 1).reshape(4, rows, half)
    state = jnp.stack([own, own, jnp.zeros_like(own)])
    gains = chunks.reshape(2, n, 2 * rows, half)
    basis = legendre_basis(SPECTRAL_BINS)
    local = lax.dynamic_slice_in_dim(basis, lax.axis_index("ch") * n_chan, n_chan, 0)
    wide = jnp.broadcast_to(local.T[:, :, None], (4, n_chan, half))
    ids_t = stations.T
    for iteration in range(ITERS):
        partial = local_totals(vis, model, stations, ids_t, gains, n)
        gains, state, coefs = exchange(partial, state, wide, iteration == ITERS - 1, n, n_ch)
    out = gains.reshape(2, n, 2, rows, half).transpose(2, 1, 3, 0, 4)
    out = out.reshape(initial_gains.shape)
    coefs = coefs.reshape(2, n, 4, 2, per, half).transpose(3, 1, 4, 2, 0, 5)
    coefs = coefs.reshape(2, n_dir, 4, 1, n_st)
    consensus = sum(coefs[:, :, k] * local[None, None, :, k, None] for k in range(4))
    return out, consensus


def solution(mesh):
    placed = (
        P(None, "ch", "bl"),
        P(None, None, "ch", "bl"),
        P(None, "bl"),
        P(None, None, "ch", None),
    )
    return jax.shard_map(
        functools.partial(per_device, mesh.shape["bl"], mesh.shape["ch"]),
        mesh=mesh,
        in_specs=placed,
        out_specs=(P(None, None, "ch", None), P(None, None, "ch", None)),
        check_vma=False,
    )
```

profile of v0, /device:TPU:5, one launch (start us, length us, event | category | flops | bytes accessed | tf_op | source)
XLA Modules:
  0.0 168.9 jit_solution(2131279732738622698)
XLA Ops:
  0.6 0.6 multiply_reduce_fusion.8
  1.2 0.6 multiply_reduce_fusion.6
  1.9 0.7 multiply_reduce_fusion.3
  6.5 1.3 multiply_reduce_fusion.2
  8.6 2.0 %multiply_reduce_fusion.1 = (f32[]{:T(128)}, f32[64]{0:T(128)S(1)}) fusion(f32[64]{0:T(128)S(1)} %get-tuple-element.22, f32[]{:T(128)} %get-tuple-element.14, f32[]{:T(128)S(6)} %mul.185, f32[]{:T(128)S(6)} %sqrt.11, f32[]{:T(128)} %get-tuple-element.21, f32[]{:T(128)S(6)} %mul.177), kind=kLoop, calls=%fused_computation.19 | loop fusion | flops 831 | bytes 536 | tf_op jit(solution)/shard_map/reduce_sum | solution.py:24
  10.6 1.9 %multiply_reduce_fusion = f32[]{:T(128)} fusion(f32[64]{0:T(128)S(1)} %get-tuple-element.20, f32[]{:T(128)} %get-tuple-element.19, f32[64]{0:T(128)S(1)} %get-tuple-element.22, f32[]{:T(128)} %get-tuple-element.14, f32[]{:T(128)S(6)} %mul.185), kind=kLoop, calls=%fused_computation.18 | loop fusion | flops 703 | bytes 528 | tf_op jit(solution)/shard_map/reduce_sum | solution.py:25
  13.1 2.0 %fusion.5 = (f32[64,1]{0,1:T(1,128)S(1)}, f32[64,1]{0,1:T(1,128)S(1)}, f32[64,1]{0,1:T(1,128)S(1)}) fusion(f32[]{:T(128)S(6)} %sqrt.12, f32[]{:T(128)} %get-tuple-element.19, f32[]{:T(128)} %get-tuple-element.14, f32[]{:T(128)S(6)} %mul.185, f32[]{:T(128)S(6)} %sqrt.11, f32[]{:T(128)} %get-tuple-element.21, f32[]{:T(128)S(6)} %mul.177, f32[]{:T(128)S(6)} %sqrt.10, ...), kind=kLoop, calls=%fused_computation.35 | loop fusion | flops 1024 | bytes 804 | tf_op jit(solution)/shard_map/div | solution.py:25
  15.4 1.9 %reshape.97 = f32[2,8,32,2,256]{4,3,2,1,0:T(2,128)S(1)} reshape(f32[2,16,16,512]{3,2,1,0:T(8,128)} %param.7) | data formatting | bytes 2097152 | tf_op jit(solution)/shard_map/reshape | solution.py:380
  17.4 1.1 copy.11
  18.6 1.3 copy.10
  19.9 19.9 %station_totals.3 = f32[2,8,96,256]{3,2,1,0:T(8,128)} custom-call(f32[2,16,2048]{2,1,0:T(8,128)} %vis_ref.5, f32[2,16,16,2048]{3,2,1,0:T(8,128)} %model_ref.5, s32[2,2048]{1,0:T(2,128)} %row_ref.5, s32[2048,2]{1,0:T(8,128)} %bitcast.48, f32[2,8,64,256]{3,2,1,0:T(8,128)} %bitcast.51), custom_call_target="tpu_custom_call" | custom-call | tf_op jit(solution)/shard_map/station_totals/pallas_call | solution.py:121
  39.9 1.4 copy-done.1
  41.3 26.0 %exchange.2 = (f32[2,2,2,2,64,256]{5,4,3,2,1,0:T(8,128)S(1)}, f32[3,4,32,256]{3,2,1,0:T(8,128)S(1)}, f32[2,1,1,1,4,4,256]{6,5,4,3,2,1,0:T(4,128)}) custom-call(f32[2,2,2,2,96,256]{5,4,3,2,1,0:T(8,128)S(1)} %bitcast.43, f32[3,4,32,256]{3,2,1,0:T(8,128)S(1)} %maximum_maximum_fusion.state_ref, f32[4,16,256]{2,1,0:T(8,128)S(1)} %broadcast_in_dim.2.basis_ref), custom_call_target="tpu_custom_call" | custom-call | tf_op jit(solution)/shard_map/exchange/pallas_call | solution.py:342
  67.3 1.0 copy-done.4
  68.3 19.9 %station_totals.4 = f32[2,8,96,256]{3,2,1,0:T(8,128)} custom-call(f32[2,16,2048]{2,1,0:T(8,128)} %vis_ref.5, f32[2,16,16,2048]{3,2,1,0:T(8,128)} %model_ref.5, s32[2,2048]{1,0:T(2,128)} %row_ref.5, s32[2048,2]{1,0:T(8,128)} %bitcast.49, f32[2,8,64,256]{3,2,1,0:T(8,128)} %bitcast.47), custom_call_target="tpu_custom_call" | custom-call | tf_op jit(solution)/shard_map/station_totals/pallas_call | solution.py:121
  88.2 1.4 copy-done.2
  89.6 23.6 %exchange.3 = (f32[2,2,2,2,64,256]{5,4,3,2,1,0:T(8,128)S(1)}, f32[3,4,32,256]{3,2,1,0:T(8,128)S(1)}, f32[2,1,1,1,4,4,256]{6,5,4,3,2,1,0:T(4,128)}) custom-call(f32[2,2,2,2,96,256]{5,4,3,2,1,0:T(8,128)S(1)} %bitcast.44, f32[3,4,32,256]{3,2,1,0:T(8,128)S(1)} %get-tuple-element.9.state_ref, f32[4,16,256]{2,1,0:T(8,128)S(1)} %broadcast_in_dim.2.basis_ref), custom_call_target="tpu_custom_call" | custom-call | tf_op jit(solution)/shard_map/exchange/pallas_call | solution.py:342
  113.2 1.0 copy-done.3
  114.2 19.9 %station_totals.5 = f32[2,8,96,256]{3,2,1,0:T(8,128)} custom-call(f32[2,16,2048]{2,1,0:T(8,128)} %vis_ref.5, f32[2,16,16,2048]{3,2,1,0:T(8,128)} %model_ref.5, s32[2,2048]{1,0:T(2,128)} %row_ref.5, s32[2048,2]{1,0:T(8,128)} %bitcast.50, f32[2,8,64,256]{3,2,1,0:T(8,128)} %bitcast.46), custom_call_target="tpu_custom_call" | custom-call | tf_op jit(solution)/shard_map/station_totals/pallas_call | solution.py:121
  134.1 1.4 copy-done
  135.5 28.7 %exchange_last.1 = (f32[2,2,2,2,64,256]{5,4,3,2,1,0:T(8,128)S(1)}, f32[3,4,32,256]{3,2,1,0:T(8,128)}, f32[2,2,2,2,4,4,256]{6,5,4,3,2,1,0:T(4,128)S(1)}) custom-call(f32[2,2,2,2,96,256]{5,4,3,2,1,0:T(8,128)S(1)} %bitcast.42, f32[3,4,32,256]{3,2,1,0:T(8,128)S(1)} %get-tuple-element.11.state_ref, f32[4,16,256]{2,1,0:T(8,128)S(1)} %broadcast_in_dim.2.basis_ref), custom_call_target="tpu_custom_call" | custom-call | tf_op jit(solution)/shard_map/exchange_last/pallas_call | solution.py:342
  164.3 0.8 copy.13
  165.1 1.8 %reshape.104 = f32[2,16,16,512]{3,2,1,0:T(8,128)} reshape(f32[2,8,32,2,256]{4,3,2,1,0:T(2,128)S(1)} %copy.13) | data formatting | bytes 2097152 | tf_op jit(solution)/shard_map/reshape | solution.py:393
  167.6 1.3 multiply_add_fusion
  (23 shorter events, 2.4 us)
Async XLA Ops:
  17.3 1.3 copy-start.5
  39.9 1.4 copy-start.1
  67.3 1.0 copy-start.4
  88.2 1.4 copy-start.2
  113.2 1.0 copy-start.3
  134.1 1.4 copy-start
where the time goes:
time: 169 us
  Pallas kernels  138 us (82%)
  local copies, waits for them, and re-layouts  14.1 us (8%)
  other arithmetic  11.9 us (7%)
  between operations  4.79 us (3%)
    pallas_call x3, Pallas kernels, exchange(): pl.pallas_call(body, out_shape=(jax.ShapeDtypeStruct((2,) + twos + (2 * r...  78.4 us
    pallas_call x3, Pallas kernels, local_totals(): pl.pallas_call(functools.partial(totals_kernel, n_chunks, n_dir, n_chan),...  59.7 us
    unnamed x14, local copies, waits for them, and re-layouts  7.52 us
    reduce_sum x6, other arithmetic, legendre_basis(): vector = vector - jnp.sum(earlier * vector) * earlier  5.84 us

commit v1 on v0

--- a/solution.py
+++ b/solution.py
@@ -16,15 +16,16 @@
 
 
 def legendre_basis(channel_count):
-    abscissa = -1.0 + 2.0 * jnp.arange(channel_count, dtype=jnp.float32) / (channel_count - 1)
+    steps = np.arange(channel_count, dtype=np.float32)
+    abscissa = np.float32(-1.0) + np.float32(2.0) * steps / np.float32(channel_count - 1)
     columns = []
     for degree in range(4):
         vector = abscissa**degree
         for earlier in columns:
-            vector = vector - jnp.sum(earlier * vector) * earlier
-        vector = vector / jnp.sqrt(jnp.sum(vector * vector))
-        columns.append(vector)
-    return jnp.stack(columns, axis=1)
+            vector = vector - np.sum(earlier * vector) * earlier
+        vector = vector / np.sqrt(np.sum(vector * vector))
+        columns.append(vector.astype(np.float32))
+    return jnp.asarray(np.stack(columns, axis=1))
 
 
 def split(value):
@@ -56,6 +57,8 @@
     station = lax.broadcasted_iota(jnp.int32, (n_st, block), 0)
     hot_l = (station == row_ref[0:1, :]).astype(jnp.float32).astype(jnp.bfloat16)
     hot_r = (station == row_ref[1:2, :]).astype(jnp.float32).astype(jnp.bfloat16)
+    for side, hot in enumerate((hot_l, hot_r)):
+        back[:, pl.ds(pl.multiple_of((step * 2 + side) * block, 128), block)] = hot
     for hot, gain in ((hot_l, gain_l), (hot_r, gain_r)):
         both = jnp.dot(pieces[...], hot, preferred_element_type=jnp.float32)
         gain[...] = both[: 2 * rows] + both[2 * rows :]
@@ -93,15 +96,11 @@
                 terms[pl.ds(base, n_chan), pl.ds(pl.multiple_of((step * 2 + side) * block, 128), block)] = high
                 terms[pl.ds(3 * rows + base, n_chan), pl.ds(pl.multiple_of((step * 2 + side) * block, 128), block)] = low
 
-    ids = lax.broadcasted_iota(jnp.int32, (block, n_st), 1)
-    back_l = (ids == col_ref[:, 0:1]).astype(jnp.float32).astype(jnp.bfloat16)
-    back_r = (ids == col_ref[:, 1:2]).astype(jnp.float32).astype(jnp.bfloat16)
-    back[pl.ds(step * 2 * block, block), :] = back_l
-    back[pl.ds(step * 2 * block + block, block), :] = back_r
-
     @pl.when(step == pl.num_programs(0) - 1)
     def _():
-        accum[...] = jnp.dot(terms[...], back[...], preferred_element_type=jnp.float32)
+        accum[...] = lax.dot_general(
+            terms[...], back[...], (((1,), (1,)), ((), ())), preferred_element_type=jnp.float32
+        )
         for h in range(2):
             for c in range(n_chunks):
                 for q in range(3):
@@ -135,7 +134,7 @@
             pltpu.VMEM((2 * rows, block), jnp.float32),
             pltpu.VMEM((2 * rows, block), jnp.float32),
             pltpu.VMEM((6 * rows, 2 * n_base), jnp.bfloat16),
-            pltpu.VMEM((2 * n_base, n_st), jnp.bfloat16),
+            pltpu.VMEM((n_st, 2 * n_base), jnp.bfloat16),
             pltpu.VMEM((6 * rows, n_st), jnp.float32),
         ],
         compiler_params=pltpu.CompilerParams(vmem_limit_bytes=56 * 2**20),

time: 169 us -> 155 us (0.917)
  other arithmetic: 11.9 us -> 1.41 us
  between operations: 4.79 us -> 0.75 us
    reduce_sum x8 -> x0, other arithmetic: 8.39 us -> none  [the longest x6 5.84 us: legendre_basis(): vector = vector - jnp.sum(earlier * vector) * earlier]
    div x1 -> x0, other arithmetic: 2 us -> none  [legendre_basis(): vector = vector / jnp.sqrt(jnp.sum(vector * vector))]
where the time goes in v1:
time: 155 us; the launch traced here: 154 us
  Pallas kernels  138 us (89%)
  local copies, waits for them, and re-layouts  14.7 us (9%)
    pallas_call x3, Pallas kernels, exchange(): pl.pallas_call(body, out_shape=(jax.ShapeDtypeStruct((2,) + twos + (2 * r...  78.5 us
    pallas_call x3, Pallas kernels, local_totals(): pl.pallas_call(functools.partial(totals_kernel, n_chunks, n_dir, n_chan),...  59.1 us
    unnamed x14, local copies, waits for them, and re-layouts  7.52 us

profile of v1, /device:TPU:5, one launch (start us, length us, event | category | flops | bytes accessed | tf_op | source)
XLA Modules:
  0.0 154.5 jit_solution(15271974894644039558)
XLA Ops:
  0.6 0.1 pad.2.clone
  0.7 0.8 constant_dynamic-slice_fusion
  1.5 0.1 broadcast_in_dim.2.basis_ref
  1.5 1.9 %reshape.43 = f32[2,8,32,2,256]{4,3,2,1,0:T(2,128)S(1)} reshape(f32[2,16,16,512]{3,2,1,0:T(8,128)} %param.8) | data formatting | bytes 2097152 | tf_op jit(solution)/shard_map/reshape | solution.py:379
  3.5 1.1 copy.12
  4.6 0.1 maximum_maximum_fusion.state_ref
  4.7 1.3 copy.11
  6.1 19.7 %station_totals.3 = f32[2,8,96,256]{3,2,1,0:T(8,128)} custom-call(f32[2,16,2048]{2,1,0:T(8,128)} %vis_ref.5, f32[2,16,16,2048]{3,2,1,0:T(8,128)} %model_ref.5, s32[2,2048]{1,0:T(2,128)} %row_ref.5, s32[2048,2]{1,0:T(8,128)} %bitcast.47, f32[2,8,64,256]{3,2,1,0:T(8,128)} %bitcast.50), custom_call_target="tpu_custom_call" | custom-call | tf_op jit(solution)/shard_map/station_totals/pallas_call | solution.py:120
  25.8 1.4 copy-done.1
  27.2 26.0 %exchange.2 = (f32[2,2,2,2,64,256]{5,4,3,2,1,0:T(8,128)S(1)}, f32[3,4,32,256]{3,2,1,0:T(8,128)S(1)}, f32[2,1,1,1,4,4,256]{6,5,4,3,2,1,0:T(4,128)}) custom-call(f32[2,2,2,2,96,256]{5,4,3,2,1,0:T(8,128)S(1)} %bitcast.42, f32[3,4,32,256]{3,2,1,0:T(8,128)S(1)} %maximum_maximum_fusion.state_ref, f32[4,16,256]{2,1,0:T(8,128)S(1)} %broadcast_in_dim.2.basis_ref), custom_call_target="tpu_custom_call" | custom-call | tf_op jit(solution)/shard_map/exchange/pallas_call | solution.py:341
  53.2 1.0 copy-done.4
  54.2 19.7 %station_totals.4 = f32[2,8,96,256]{3,2,1,0:T(8,128)} custom-call(f32[2,16,2048]{2,1,0:T(8,128)} %vis_ref.5, f32[2,16,16,2048]{3,2,1,0:T(8,128)} %model_ref.5, s32[2,2048]{1,0:T(2,128)} %row_ref.5, s32[2048,2]{1,0:T(8,128)} %bitcast.48, f32[2,8,64,256]{3,2,1,0:T(8,128)} %bitcast.46), custom_call_target="tpu_custom_call" | custom-call | tf_op jit(solution)/shard_map/station_totals/pallas_call | solution.py:120
  73.9 1.4 copy-done.2
  75.3 23.7 %exchange.3 = (f32[2,2,2,2,64,256]{5,4,3,2,1,0:T(8,128)S(1)}, f32[3,4,32,256]{3,2,1,0:T(8,128)S(1)}, f32[2,1,1,1,4,4,256]{6,5,4,3,2,1,0:T(4,128)}) custom-call(f32[2,2,2,2,96,256]{5,4,3,2,1,0:T(8,128)S(1)} %bitcast.43, f32[3,4,32,256]{3,2,1,0:T(8,128)S(1)} %get-tuple-element.9.state_ref, f32[4,16,256]{2,1,0:T(8,128)S(1)} %broadcast_in_dim.2.basis_ref), custom_call_target="tpu_custom_call" | custom-call | tf_op jit(solution)/shard_map/exchange/pallas_call | solution.py:341
  98.9 1.0 copy-done.3
  99.9 19.7 %station_totals.5 = f32[2,8,96,256]{3,2,1,0:T(8,128)} custom-call(f32[2,16,2048]{2,1,0:T(8,128)} %vis_ref.5, f32[2,16,16,2048]{3,2,1,0:T(8,128)} %model_ref.5, s32[2,2048]{1,0:T(2,128)} %row_ref.5, s32[2048,2]{1,0:T(8,128)} %bitcast.49, f32[2,8,64,256]{3,2,1,0:T(8,128)} %bitcast.45), custom_call_target="tpu_custom_call" | custom-call | tf_op jit(solution)/shard_map/station_totals/pallas_call | solution.py:120
  119.6 1.4 copy-done
  121.0 28.8 %exchange_last.1 = (f32[2,2,2,2,64,256]{5,4,3,2,1,0:T(8,128)S(1)}, f32[3,4,32,256]{3,2,1,0:T(8,128)}, f32[2,2,2,2,4,4,256]{6,5,4,3,2,1,0:T(4,128)S(1)}) custom-call(f32[2,2,2,2,96,256]{5,4,3,2,1,0:T(8,128)S(1)} %bitcast.41, f32[3,4,32,256]{3,2,1,0:T(8,128)S(1)} %get-tuple-element.11.state_ref, f32[4,16,256]{2,1,0:T(8,128)S(1)} %broadcast_in_dim.2.basis_ref), custom_call_target="tpu_custom_call" | custom-call | tf_op jit(solution)/shard_map/exchange_last/pallas_call | solution.py:341
  149.8 0.8 copy.14
  150.7 1.8 %reshape.50 = f32[2,16,16,512]{3,2,1,0:T(8,128)} reshape(f32[2,8,32,2,256]{4,3,2,1,0:T(2,128)S(1)} %copy.14) | data formatting | bytes 2097152 | tf_op jit(solution)/shard_map/reshape | solution.py:392
  152.5 0.2 reshape.51
  152.7 0.2 copy.18
  152.9 0.2 reshape.52
  153.1 1.3 multiply_add_fusion
  (11 shorter events, 0.1 us)
Async XLA Ops:
  3.4 1.3 copy-start.5
  25.8 1.4 copy-start.1
  53.2 1.0 copy-start.4
  73.9 1.4 copy-start.2
  98.9 1.0 copy-start.3
  119.6 1.4 copy-start
